TPU v7x, 32 devices: a whole 2x2x4 slice. The times are simulated.
32 devices in a mesh: groups: 2 (over x), spatial: 16 (over z, y, core).
Axes of the slice: x: 2, y: 2, z: 4, core: 2. Of those that a mesh axis runs over, the one named last changes fastest.
Arguments:
- fields: bfloat16 [1024, 128, 768], P(('groups', 'spatial')), parts along dimension 0, may hold values from -6 to 6
- norm1_gain: float32 [768], replicated, may hold values from 0.5 to 1.5
- norm1_bias: float32 [768], replicated, may hold values from -3 to 3
- spectral_w1: float32 [2, 8, 96, 96], replicated, may hold values from -0.4375 to 0.4375
- spectral_b1: float32 [2, 8, 96], replicated, may hold values from -3 to 3
- spectral_w2: float32 [2, 8, 96, 96], replicated, may hold values from -0.4375 to 0.4375
- spectral_b2: float32 [2, 8, 96], replicated, may hold values from -3 to 3
- norm2_gain: float32 [768], replicated, may hold values from 0.5 to 1.5
- norm2_bias: float32 [768], replicated, may hold values from -3 to 3
- fc1_weight: bfloat16 [768, 3072], replicated, may hold values from -0.21875 to 0.21875
- fc1_bias: float32 [3072], replicated, may hold values from -3 to 3
- fc2_weight: bfloat16 [3072, 768], replicated, may hold values from -0.109375 to 0.109375
- fc2_bias: float32 [768], replicated, may hold values from -3 to 3
Outputs:
- next_state: bfloat16 [1024, 128, 768], P(('groups', 'spatial')), parts along dimension 0
- anomaly: bfloat16 [1024, 128, 768], P(('groups', 'spatial')), parts along dimension 0
There are 2 independent parts, one for each index of `groups`. A program takes and returns all parts, laid end to end along the dimension named above; an argument that names none is the same for every part. Nothing has to cross between parts.
All inputs are finite; a program needn't handle non-finite values.
Results may differ from a plain program's by a relative error of at most 0.0056.
Values may be sent and summed in bfloat16 or wider, within the bound.
A program may use at most 192 MiB of HBM per device.

v0:
```python
import math
import jax
import jax.numpy as jnp
from jax import lax
from jax.sharding import PartitionSpec as P

MEMBERS = 8
EPSILON = 1e-06
SHRINK = 0.01
FULL_PRECISION = lax.Precision.HIGHEST


def from_behind(block, axis, distance):
    devices = range(lax.axis_size(axis))
    route = [((i - distance) % len(devices), i) for i in devices]
    return lax.ppermute(block, axis, route)


def layer_norm(values, gain, offset_term):
    center = values - jnp.mean(values, axis=-1, keepdims=True)
    spread = jnp.mean(center * center, axis=-1, keepdims=True)
    return center * lax.rsqrt(spread + EPSILON) * gain + offset_term


def soft_shrink(values):
    return jnp.where(
        values > SHRINK, values - SHRINK, jnp.where(values < -SHRINK, values + SHRINK, 0.0)
    )


def contract(form, left, right):
    return jnp.einsum(form, left, right, precision=FULL_PRECISION)


def block_product(values, weight):
    return jnp.einsum("...bi,bio->...bo", values, weight, precision=FULL_PRECISION)


def angle_table(first_len, second_len, modulus):
    first_index = lax.broadcasted_iota(jnp.int32, (first_len, second_len), 0)
    second_index = lax.broadcasted_iota(jnp.int32, (first_len, second_len), 1)
    phase = first_index * second_index % modulus
    return phase.astype(jnp.float32) * (2.0 * math.pi / modulus)


def spectral_layer(real_part, imag_part, w_first, b_first, w_second, b_second):
    shape = real_part.shape
    block_count = w_first.shape[1]
    split_shape = shape[:-1] + (block_count, shape[-1] // block_count)
    real_part = real_part.reshape(split_shape)
    imag_part = imag_part.reshape(split_shape)
    hidden_real = jax.nn.relu(
        block_product(real_part, w_first[0]) - block_product(imag_part, w_first[1]) + b_first[0]
    )
    hidden_imag = jax.nn.relu(
        block_product(imag_part, w_first[0]) + block_product(real_part, w_first[1]) + b_first[1]
    )
    mixed_real = (
        block_product(hidden_real, w_second[0])
        - block_product(hidden_imag, w_second[1])
        + b_second[0]
    )
    mixed_imag = (
        block_product(hidden_imag, w_second[0])
        + block_product(hidden_real, w_second[1])
        + b_second[1]
    )
    return (soft_shrink(mixed_real).reshape(shape), soft_shrink(mixed_imag).reshape(shape))


def longitude_forward(normed, lon_len):
    angles = angle_table(lon_len, lon_len // 2, lon_len)
    factor = 1.0 / math.sqrt(lon_len)
    real_part = contract("rld,lk->rkd", normed, jnp.cos(angles) * factor)
    imag_part = -contract("rld,lk->rkd", normed, jnp.sin(angles) * factor)
    return (real_part, imag_part)


def longitude_inverse(real_part, imag_part, lon_len):
    half_len = lon_len // 2
    angles = angle_table(lon_len, half_len, lon_len)
    column_index = lax.broadcasted_iota(jnp.int32, (1, half_len), 1)
    weights = jnp.where(column_index == 0, 1.0, 2.0) / math.sqrt(lon_len)
    cosine_table = jnp.cos(angles) * weights
    sine_table = jnp.sin(angles) * weights
    return contract("rkd,lk->rld", real_part, cosine_table) - contract(
        "rkd,lk->rld", imag_part, sine_table
    )


def latitude_work(real_part, imag_part, w_first, b_first, w_second, b_second):
    member_rows, mode_count, channels = real_part.shape
    lat_len = member_rows // MEMBERS
    angles = angle_table(lat_len, lat_len, lat_len)
    factor = 1.0 / math.sqrt(lat_len)
    cosine_table = jnp.cos(angles) * factor
    sine_table = jnp.sin(angles) * factor
    grid_real = real_part.reshape(MEMBERS, lat_len, mode_count, channels)
    grid_imag = imag_part.reshape(MEMBERS, lat_len, mode_count, channels)
    spec_real = contract("qp,mpkd->mqkd", cosine_table, grid_real) + contract(
        "qp,mpkd->mqkd", sine_table, grid_imag
    )
    spec_imag = contract("qp,mpkd->mqkd", cosine_table, grid_imag) - contract(
        "qp,mpkd->mqkd", sine_table, grid_real
    )
    mixed_real, mixed_imag = spectral_layer(
        spec_real, spec_imag, w_first, b_first, w_second, b_second
    )
    back_real = contract("qp,mpkd->mqkd", cosine_table, mixed_real) - contract(
        "qp,mpkd->mqkd", sine_table, mixed_imag
    )
    back_imag = contract("qp,mpkd->mqkd", cosine_table, mixed_imag) + contract(
        "qp,mpkd->mqkd", sine_table, mixed_real
    )
    return (
        back_real.reshape(member_rows, mode_count, channels),
        back_imag.reshape(member_rows, mode_count, channels),
    )


def on_device(
    fields,
    norm1_gain,
    norm1_bias,
    spectral_w1,
    spectral_b1,
    spectral_w2,
    spectral_b2,
    norm2_gain,
    norm2_bias,
    fc1_weight,
    fc1_bias,
    fc2_weight,
    fc2_bias,
):
    row_count, lon_len, channels = fields.shape
    state = fields.astype(jnp.float32)
    normed = layer_norm(state, norm1_gain, norm1_bias)
    real_part, imag_part = longitude_forward(normed, lon_len)
    real_part, imag_part = (
        lax.all_to_all(real_part, "spatial", split_axis=1, concat_axis=0, tiled=True),
        lax.all_to_all(imag_part, "spatial", split_axis=1, concat_axis=0, tiled=True),
    )
    real_part, imag_part = latitude_work(
        real_part, imag_part, spectral_w1, spectral_b1, spectral_w2, spectral_b2
    )
    real_part, imag_part = (
        lax.all_to_all(real_part, "spatial", split_axis=0, concat_axis=1, tiled=True),
        lax.all_to_all(imag_part, "spatial", split_axis=0, concat_axis=1, tiled=True),
    )
    filtered = longitude_inverse(real_part, imag_part, lon_len)
    residual = (filtered + normed + state).reshape(row_count * lon_len, channels)
    normed2 = layer_norm(residual, norm2_gain, norm2_bias).astype(jnp.bfloat16)
    hidden = jax.nn.gelu(
        jnp.dot(normed2, fc1_weight, preferred_element_type=jnp.float32) + fc1_bias,
        approximate=False,
    ).astype(jnp.bfloat16)
    updated = residual + jnp.dot(hidden, fc2_weight, preferred_element_type=jnp.float32) + fc2_bias
    next_state = updated.astype(jnp.bfloat16).reshape(row_count, lon_len, channels)
    device_count = lax.axis_size("spatial")
    member_span = device_count // MEMBERS
    state_values = next_state.astype(jnp.float32)

    def advance(counter, state_pair):
        moving, summed = state_pair
        moving = from_behind(moving, "spatial", member_span)
        return (moving, summed + moving.astype(jnp.float32))

    ignored, summed = lax.fori_loop(0, MEMBERS - 1, advance, (next_state, state_values))
    ensemble_mean = summed / MEMBERS
    anomaly = (state_values - ensemble_mean).astype(jnp.bfloat16)
    return (next_state, anomaly)


def solution(mesh):
    placed = (
        P(("groups", "spatial"), None, None),
        P(),
        P(),
        P(),
        P(),
        P(),
        P(),
        P(),
        P(),
        P(),
        P(),
        P(),
        P(),
    )
    return jax.shard_map(
        on_device,
        mesh=mesh,
        in_specs=placed,
        out_specs=(P(("groups", "spatial"), None, None), P(("groups", "spatial"), None, None)),
        check_vma=False,
    )
```

profile of v0, /device:TPU:0, one launch (start us, length us, event | category | flops | bytes accessed | tf_op | source)
XLA Modules:
  0.0 2131.6 jit_solution(12978921306262983575)
XLA Ops:
  7.6 9.6 negate_bitcast_fusion
  17.2 6.6 copy.58
  23.8 7.5 all-to-all-start.1
  31.3 12.0 fusion.94
  43.3 6.3 copy.55
  49.6 95.7 %all-to-all-done.1 = f32[32,64,768]{2,0,1:T(8,128)} async-done(((f32[32,64,768]{2,0,1:T(8,128)}), f32[32,64,768]{2,0,1:T(8,128)}, u32[]{:S(2)}, u32[]{:S(2)}) %all-to-all-start.1) | async-done | bytes 6291488 | tf_op jit(solution)/shard_map/all_to_all | solution.py:142
  145.3 28.5 %all-to-all-start = ((f32[32,64,768]{2,0,1:T(8,128)}), f32[32,64,768]{2,0,1:T(8,128)}, u32[]{:S(2)}, u32[]{:S(2)}) async-start(f32[32,64,768]{2,0,1:T(8,128)} %copy.55), calls=%async_computation | async-start | bytes 12582912 | tf_op jit(solution)/shard_map/all_to_all | solution.py:141
  177.4 7.9 fusion.74
  185.3 7.8 fusion.76
  193.1 94.8 %all-to-all-done = f32[32,64,768]{2,0,1:T(8,128)} async-done(((f32[32,64,768]{2,0,1:T(8,128)}), f32[32,64,768]{2,0,1:T(8,128)}, u32[]{:S(2)}, u32[]{:S(2)}) %all-to-all-start) | async-done | bytes 6291488 | tf_op jit(solution)/shard_map/all_to_all | solution.py:141
  294.3 7.9 subtract_bitcast_fusion.1
  302.2 9.9 reshape.102
  312.1 13.7 fusion.58
  325.9 9.9 fusion.60
  335.7 8.2 add_bitcast_fusion.1
  343.9 9.9 reshape.101
  353.8 13.1 add_maximum_fusion
  367.0 9.5 fusion.50
  376.4 9.8 fusion.52
  386.3 9.6 add_maximum_fusion.1
  395.9 14.9 select_bitcast_fusion
  410.8 11.0 copy.68
  421.8 9.6 reshape.104
  431.4 12.2 select_bitcast_fusion.1
  443.7 11.0 copy.67
  454.7 9.6 reshape.103
  464.2 8.3 fusion.128
  472.5 8.7 subtract_bitcast_fusion
  481.8 6.6 copy.70
  488.4 28.3 %all-to-all-start.2 = ((f32[512,4,768]{2,1,0:T(4,128)}), f32[512,4,768]{2,1,0:T(4,128)}, u32[]{:S(2)}, u32[]{:S(2)}) async-start(f32[512,4,768]{2,1,0:T(4,128)} %copy.70), calls=%async_computation.2 | async-start | bytes 12582912 | tf_op jit(solution)/shard_map/all_to_all | solution.py:148
  516.7 8.6 fusion.126
  525.3 6.7 add_bitcast_fusion
  532.5 6.7 copy.74
  539.2 91.5 %all-to-all-done.2 = f32[512,4,768]{2,1,0:T(4,128)} async-done(((f32[512,4,768]{2,1,0:T(4,128)}), f32[512,4,768]{2,1,0:T(4,128)}, u32[]{:S(2)}, u32[]{:S(2)}) %all-to-all-start.2) | async-done | bytes 6291488 | tf_op jit(solution)/shard_map/all_to_all | solution.py:148
  630.7 28.5 %all-to-all-start.3 = ((f32[512,4,768]{2,1,0:T(4,128)}), f32[512,4,768]{2,1,0:T(4,128)}, u32[]{:S(2)}, u32[]{:S(2)}) async-start(f32[512,4,768]{2,1,0:T(4,128)} %copy.74), calls=%async_computation.3 | async-start | bytes 12582912 | tf_op jit(solution)/shard_map/all_to_all | solution.py:149
  663.3 6.7 copy.72
  670.0 7.7 all_to_all.57
  677.7 95.6 %all-to-all-done.3 = f32[512,4,768]{2,1,0:T(4,128)} async-done(((f32[512,4,768]{2,1,0:T(4,128)}), f32[512,4,768]{2,1,0:T(4,128)}, u32[]{:S(2)}, u32[]{:S(2)}) %all-to-all-start.3) | async-done | bytes 6291488 | tf_op jit(solution)/shard_map/all_to_all | solution.py:149
  777.3 6.7 copy.76
  784.1 7.9 all_to_all.61
  792.0 15.1 fusion.134
  807.1 19.1 fusion.262
  830.9 126.4 %fusion.2.clone.6 = bf16[4096,3072]{1,0:T(8,128)(2,1)} fusion(bf16[4096,768]{1,0:T(8,128)(2,1)S(1)} %fusion.47, bf16[768,3072]{1,0:T(8,128)(2,1)} %param.24, f32[3072]{0:T(1024)S(1)} %copy-done.22), kind=kOutput, calls=%fused_computation.4.clone.clone.clone.clone.clone.1 | convolution fusion | flops 20157825024 | bytes 36188160 | tf_op jit(solution)/shard_map/dot_general | solution.py:155
  957.2 26.3 %fusion.49 = bf16[4096,768]{1,0:T(8,128)(2,1)S(1)} fusion(f32[32,128,768]{2,1,0:T(8,128)} %copy-done, bf16[3072,768]{1,0:T(8,128)(2,1)} %param.26, f32[768]{0:T(1024)S(1)} %copy-done.23, bf16[4096,3072]{1,0:T(8,128)(2,1)} %fusion.2.clone.6), kind=kOutput, calls=%fused_computation.62 | convolution fusion | flops 19336790016 | bytes 48761856 | tf_op jit(solution)/shard_map/dot_general | solution.py:158
  992.4 1127.6 %while.12 = (s32[]{:T(128)}, bf16[32,128,768]{2,1,0:T(8,128)(2,1)}, f32[32,128,768]{2,1,0:T(8,128)}, s32[]{:T(128)}) while((s32[]{:T(128)}, bf16[32,128,768]{2,1,0:T(8,128)(2,1)}, f32[32,128,768]{2,1,0:T(8,128)}, s32[]{:T(128)}) %tuple.26), condition=%wide.region_5.6_spmd, body=%wide.region_4.5_spmd.sunk | while | flops 6291458 | bytes 69206104 | solution.py:169
  992.6 9.1 collective-permute-start
  1001.7 154.1 %collective-permute-done = bf16[32,128,768]{2,1,0:T(8,128)(2,1)} collective-permute-done((bf16[32,128,768]{2,1,0:T(8,128)(2,1)}, bf16[32,128,768]{2,1,0:T(8,128)(2,1)}, u32[]{:S(2)}, u32[]{:S(2)}) %collective-permute-start) | collective-permute-done | bytes 6291488 | tf_op jit(solution)/shard_map/while/body/eval_jaxpr/ppermute | solution.py:16
  1155.7 6.1 copy.114
  1161.9 13.2 convert_add_fusion.3
  1175.1 140.2 %collective-permute-done = bf16[32,128,768]{2,1,0:T(8,128)(2,1)} collective-permute-done((bf16[32,128,768]{2,1,0:T(8,128)(2,1)}, bf16[32,128,768]{2,1,0:T(8,128)(2,1)}, u32[]{:S(2)}, u32[]{:S(2)}) %collective-permute-start) | collective-permute-done | bytes 6291488 | tf_op jit(solution)/shard_map/while/body/eval_jaxpr/ppermute | solution.py:16
  1315.3 6.1 copy.114
  1321.5 13.2 convert_add_fusion.3
  1334.7 139.4 %collective-permute-done = bf16[32,128,768]{2,1,0:T(8,128)(2,1)} collective-permute-done((bf16[32,128,768]{2,1,0:T(8,128)(2,1)}, bf16[32,128,768]{2,1,0:T(8,128)(2,1)}, u32[]{:S(2)}, u32[]{:S(2)}) %collective-permute-start) | collective-permute-done | bytes 6291488 | tf_op jit(solution)/shard_map/while/body/eval_jaxpr/ppermute | solution.py:16
  1474.1 6.1 copy.114
  1480.3 13.2 convert_add_fusion.3
  1493.5 138.5 %collective-permute-done = bf16[32,128,768]{2,1,0:T(8,128)(2,1)} collective-permute-done((bf16[32,128,768]{2,1,0:T(8,128)(2,1)}, bf16[32,128,768]{2,1,0:T(8,128)(2,1)}, u32[]{:S(2)}, u32[]{:S(2)}) %collective-permute-start) | collective-permute-done | bytes 6291488 | tf_op jit(solution)/shard_map/while/body/eval_jaxpr/ppermute | solution.py:16
  1638.2 13.2 convert_add_fusion.3
  1651.4 137.7 %collective-permute-done = bf16[32,128,768]{2,1,0:T(8,128)(2,1)} collective-permute-done((bf16[32,128,768]{2,1,0:T(8,128)(2,1)}, bf16[32,128,768]{2,1,0:T(8,128)(2,1)}, u32[]{:S(2)}, u32[]{:S(2)}) %collective-permute-start) | collective-permute-done | bytes 6291488 | tf_op jit(solution)/shard_map/while/body/eval_jaxpr/ppermute | solution.py:16
  1795.2 13.2 convert_add_fusion.3
  1808.4 136.8 %collective-permute-done = bf16[32,128,768]{2,1,0:T(8,128)(2,1)} collective-permute-done((bf16[32,128,768]{2,1,0:T(8,128)(2,1)}, bf16[32,128,768]{2,1,0:T(8,128)(2,1)}, u32[]{:S(2)}, u32[]{:S(2)}) %collective-permute-start) | collective-permute-done | bytes 6291488 | tf_op jit(solution)/shard_map/while/body/eval_jaxpr/ppermute | solution.py:16
  1951.4 13.2 convert_add_fusion.3
  1964.6 136.0 %collective-permute-done = bf16[32,128,768]{2,1,0:T(8,128)(2,1)} collective-permute-done((bf16[32,128,768]{2,1,0:T(8,128)(2,1)}, bf16[32,128,768]{2,1,0:T(8,128)(2,1)}, u32[]{:S(2)}, u32[]{:S(2)}) %collective-permute-start) | collective-permute-done | bytes 6291488 | tf_op jit(solution)/shard_map/while/body/eval_jaxpr/ppermute | solution.py:16
  2106.7 13.2 convert_add_fusion.3
  2120.0 11.2 subtract_convert_fusion
  (107 shorter events, 63.9 us)
Async XLA Ops:
  0.6 4.6 copy-start.3
  0.6 7.0 copy-start.16
  0.7 7.0 copy-start.18
  5.2 26.0 %copy-start.10 = (f32[32,128]{1,0:T(8,128)}, f32[32,128]{1,0:T(8,128)S(1)}, u32[]{:S(2)}) copy-start(f32[32,128]{1,0:T(8,128)S(1)} %broadcast_multiply_fusion.1) | copy-start | bytes 49156
  7.6 23.6 %copy-start.12 = (f32[32,128]{1,0:T(8,128)}, f32[32,128]{1,0:T(8,128)S(1)}, u32[]{:S(2)}) copy-start(f32[32,128]{1,0:T(8,128)S(1)} %add_rsqrt_fusion) | copy-start | bytes 49156
  23.8 121.5 %all-to-all-start.1 = ((f32[32,64,768]{2,0,1:T(8,128)}), f32[32,64,768]{2,0,1:T(8,128)}, u32[]{:S(2)}, u32[]{:S(2)}) async-start(f32[32,64,768]{2,0,1:T(8,128)} %copy.58), calls=%async_computation.1 | async-start | bytes 12582912 | tf_op jit(solution)/shard_map/all_to_all | solution.py:142
  49.6 124.2 %copy-start.14 = (f32[2,8,96]{2,1,0:T(8,128)S(1)}, f32[2,8,96]{2,1,0:T(8,128)}, u32[]{:S(2)}) copy-start(f32[2,8,96]{2,1,0:T(8,128)} %param.19) | copy-start | bytes 18436
  49.6 124.3 %copy-start.15 = (f32[2,8,96]{2,1,0:T(8,128)S(1)}, f32[2,8,96]{2,1,0:T(8,128)}, u32[]{:S(2)}) copy-start(f32[2,8,96]{2,1,0:T(8,128)} %param.21) | copy-start | bytes 18436
  145.3 142.6 %all-to-all-start = ((f32[32,64,768]{2,0,1:T(8,128)}), f32[32,64,768]{2,0,1:T(8,128)}, u32[]{:S(2)}, u32[]{:S(2)}) async-start(f32[32,64,768]{2,0,1:T(8,128)} %copy.55), calls=%async_computation | async-start | bytes 12582912 | tf_op jit(solution)/shard_map/all_to_all | solution.py:141
  193.1 101.2 %slice-start.10 = ((s8[6291456]{0:T(1024)(128)(4,1)}), s8[2097152]{0:T(1024)(128)(4,1)S(1)}, s32[]{:S(2)}) async-start(s8[6291456]{0:T(1024)(128)(4,1)} %bitcast.204), calls=%async_computation.14 | async-start | bytes 4194304
  287.9 6.4 slice-start.11
  291.6 2.7 copy-start.5
  302.2 9.9 copy-start.6
  312.1 13.7 copy-start.1
  312.1 23.6 %slice-start.4 = ((s8[6291456]{0:T(1024)(128)(4,1)}), s8[4194304]{0:T(1024)(128)(4,1)S(1)}, s32[]{:S(2)}) async-start(s8[6291456]{0:T(1024)(128)(4,1)} %bitcast.193), calls=%async_computation.8 | async-start | bytes 8388608
  312.1 23.6 %slice-start.8 = ((s8[6291456]{0:T(1024)(128)(4,1)}), s8[4194304]{0:T(1024)(128)(4,1)S(1)}, s32[]{:S(2)}) async-start(s8[6291456]{0:T(1024)(128)(4,1)} %bitcast.202), calls=%async_computation.12 | async-start | bytes 8388608
  325.8 9.9 slice-start.5
  325.9 9.9 slice-start.9
  353.8 13.2 copy-start.7
  366.9 9.5 copy-start.8
  366.9 19.3 slice-start
  367.0 19.3 slice-start.6
  376.4 9.9 slice-start.1
  376.4 9.9 slice-start.7
  395.9 14.9 copy-start.2
  421.8 9.6 copy-start.9
  488.4 36.9 %slice-start.2 = ((s8[6291456]{0:T(1024)(128)(4,1)}), s8[2097152]{0:T(1024)(128)(4,1)S(1)}, s32[]{:S(2)}) async-start(s8[6291456]{0:T(1024)(128)(4,1)} %bitcast.184), calls=%async_computation.6 | async-start | bytes 4194304
  488.4 142.3 %all-to-all-start.2 = ((f32[512,4,768]{2,1,0:T(4,128)}), f32[512,4,768]{2,1,0:T(4,128)}, u32[]{:S(2)}, u32[]{:S(2)}) async-start(f32[512,4,768]{2,1,0:T(4,128)} %copy.70), calls=%async_computation.2 | async-start | bytes 12582912 | tf_op jit(solution)/shard_map/all_to_all | solution.py:148
  516.7 8.6 slice-start.3
  630.7 142.6 %all-to-all-start.3 = ((f32[512,4,768]{2,1,0:T(4,128)}), f32[512,4,768]{2,1,0:T(4,128)}, u32[]{:S(2)}, u32[]{:S(2)}) async-start(f32[512,4,768]{2,1,0:T(4,128)} %copy.74), calls=%async_computation.3 | async-start | bytes 12582912 | tf_op jit(solution)/shard_map/all_to_all | solution.py:149
  792.0 15.2 copy-start.11
  792.0 15.2 copy-start.13
  792.0 15.2 copy-start.17
  792.0 15.2 copy-start.19
  826.3 4.6 copy-start
  826.3 1.5 copy-start.20
  826.3 1.5 copy-start.21
  827.8 3.1 copy-start.22
  830.9 126.4 %copy-start.23 = (f32[768]{0:T(1024)S(1)}, f32[768]{0:T(1024)}, u32[]{:S(2)}) copy-start(f32[768]{0:T(1024)} %param.27) | copy-start | bytes 9220
  983.5 8.9 copy-start.4
  992.6 163.1 %collective-permute-start = (bf16[32,128,768]{2,1,0:T(8,128)(2,1)}, bf16[32,128,768]{2,1,0:T(8,128)(2,1)}, u32[]{:S(2)}, u32[]{:S(2)}) collective-permute-start(bf16[32,128,768]{2,1,0:T(8,128)(2,1)} %get-tuple-element.58), channel_id=1, source_target_pairs={{14,0},{15,1},{0,2},{1,3},{2,4},{3,5},{4,6},{5,7},{6,8},{7,9},{8,1... | collective-permute-start | bytes 18874376 | tf_op jit(solution)/shard_map/while/body/eval_jaxpr/ppermute | solution.py:16
  1175.1 140.2 %collective-permute-start = (bf16[32,128,768]{2,1,0:T(8,128)(2,1)}, bf16[32,128,768]{2,1,0:T(8,128)(2,1)}, u32[]{:S(2)}, u32[]{:S(2)}) collective-permute-start(bf16[32,128,768]{2,1,0:T(8,128)(2,1)} %get-tuple-element.58), channel_id=1, source_target_pairs={{14,0},{15,1},{0,2},{1,3},{2,4},{3,5},{4,6},{5,7},{6,8},{7,9},{8,1... | collective-permute-start | bytes 18874376 | tf_op jit(solution)/shard_map/while/body/eval_jaxpr/ppermute | solution.py:16
  1334.7 139.4 %collective-permute-start = (bf16[32,128,768]{2,1,0:T(8,128)(2,1)}, bf16[32,128,768]{2,1,0:T(8,128)(2,1)}, u32[]{:S(2)}, u32[]{:S(2)}) collective-permute-start(bf16[32,128,768]{2,1,0:T(8,128)(2,1)} %get-tuple-element.58), channel_id=1, source_target_pairs={{14,0},{15,1},{0,2},{1,3},{2,4},{3,5},{4,6},{5,7},{6,8},{7,9},{8,1... | collective-permute-start | bytes 18874376 | tf_op jit(solution)/shard_map/while/body/eval_jaxpr/ppermute | solution.py:16
  1493.5 138.5 %collective-permute-start = (bf16[32,128,768]{2,1,0:T(8,128)(2,1)}, bf16[32,128,768]{2,1,0:T(8,128)(2,1)}, u32[]{:S(2)}, u32[]{:S(2)}) collective-permute-start(bf16[32,128,768]{2,1,0:T(8,128)(2,1)} %get-tuple-element.58), channel_id=1, source_target_pairs={{14,0},{15,1},{0,2},{1,3},{2,4},{3,5},{4,6},{5,7},{6,8},{7,9},{8,1... | collective-permute-start | bytes 18874376 | tf_op jit(solution)/shard_map/while/body/eval_jaxpr/ppermute | solution.py:16
  1651.4 137.7 %collective-permute-start = (bf16[32,128,768]{2,1,0:T(8,128)(2,1)}, bf16[32,128,768]{2,1,0:T(8,128)(2,1)}, u32[]{:S(2)}, u32[]{:S(2)}) collective-permute-start(bf16[32,128,768]{2,1,0:T(8,128)(2,1)} %get-tuple-element.58), channel_id=1, source_target_pairs={{14,0},{15,1},{0,2},{1,3},{2,4},{3,5},{4,6},{5,7},{6,8},{7,9},{8,1... | collective-permute-start | bytes 18874376 | tf_op jit(solution)/shard_map/while/body/eval_jaxpr/ppermute | solution.py:16
  1808.4 136.8 %collective-permute-start = (bf16[32,128,768]{2,1,0:T(8,128)(2,1)}, bf16[32,128,768]{2,1,0:T(8,128)(2,1)}, u32[]{:S(2)}, u32[]{:S(2)}) collective-permute-start(bf16[32,128,768]{2,1,0:T(8,128)(2,1)} %get-tuple-element.58), channel_id=1, source_target_pairs={{14,0},{15,1},{0,2},{1,3},{2,4},{3,5},{4,6},{5,7},{6,8},{7,9},{8,1... | collective-permute-start | bytes 18874376 | tf_op jit(solution)/shard_map/while/body/eval_jaxpr/ppermute | solution.py:16
  1964.6 136.0 %collective-permute-start = (bf16[32,128,768]{2,1,0:T(8,128)(2,1)}, bf16[32,128,768]{2,1,0:T(8,128)(2,1)}, u32[]{:S(2)}, u32[]{:S(2)}) collective-permute-start(bf16[32,128,768]{2,1,0:T(8,128)(2,1)} %get-tuple-element.58), channel_id=1, source_target_pairs={{14,0},{15,1},{0,2},{1,3},{2,4},{3,5},{4,6},{5,7},{6,8},{7,9},{8,1... | collective-permute-start | bytes 18874376 | tf_op jit(solution)/shard_map/while/body/eval_jaxpr/ppermute | solution.py:16
where the time goes:
time: 2140 us; the launch traced here: 2130 us
  waiting for transfers between devices  1360 us (64%)
  matrix products  365 us (17%)
  local copies, waits for them, and re-layouts  182 us (9%)
  other arithmetic  120 us (6%)
  starting transfers between devices  102 us (5%)
    ppermute x7, waiting for transfers between devices, from_behind(): return lax.ppermute(block, axis, route)  983 us
    dot_general x1, matrix products, on_device(): jnp.dot(normed2, fc1_weight, preferred_element_type=jnp.float32) + fc1_bias  126 us
    dot_general x12, matrix products, contract(): return jnp.einsum(form, left, right, precision=FULL_PRECISION)  120 us
    all_to_all x1, waiting for transfers between devices, on_device(): lax.all_to_all(imag_part, 'spatial', split_axis=1, concat_axis=0, tiled=T...  95.7 us
    all_to_all x1, waiting for transfers between devices, on_device(): lax.all_to_all(imag_part, 'spatial', split_axis=0, concat_axis=1, tiled=T...  95.6 us
    all_to_all x1, waiting for transfers between devices, on_device(): lax.all_to_all(real_part, 'spatial', split_axis=1, concat_axis=0, tiled=T...  94.8 us
    dot_general x8, matrix products, block_product(): jnp.einsum('...bi,bio->...bo', values, weight, precision=FULL_PRECISION)  92.7 us
    add x7, other arithmetic, advance(): return (moving, summed + moving.astype(jnp.float32))  92.6 us
  transfers between devices with their start and end apart: 11, of which 11 were waited for; matrix products, arithmetic and copies ran while one was open for 3% of the time, Pallas kernels for 0%

commit v1 on v0

--- a/solution.py
+++ b/solution.py
@@ -139,7 +139,15 @@
     real_part, imag_part = longitude_forward(normed, lon_len)
     real_part, imag_part = (
         lax.all_to_all(real_part, "spatial", split_axis=1, concat_axis=0, tiled=True),
-        lax.all_to_all(imag_part, "spatial", split_axis=1, concat_axis=0, tiled=True),
+        jnp.concatenate(
+            lax.all_to_all(
+                jnp.stack(jnp.split(imag_part, lax.axis_size("spatial"), axis=1), axis=0),
+                "spatial",
+                0,
+                0,
+            ),
+            axis=0,
+        ),
     )
     real_part, imag_part = latitude_work(
         real_part, imag_part, spectral_w1, spectral_b1, spectral_w2, spectral_b2

time: 2140 us -> 2150 us (level)
  no operation moved by 1% of the time
where the time goes in v1:
time: 2150 us; the launch traced here: 2140 us
  waiting for transfers between devices  1360 us (63%)
  matrix products  371 us (17%)
  local copies, waits for them, and re-layouts  185 us (9%)
  other arithmetic  120 us (6%)
  starting transfers between devices  102 us (5%)
    ppermute x7, waiting for transfers between devices, from_behind(): return lax.ppermute(block, axis, route)  983 us
    dot_general x1, matrix products, on_device(): jnp.dot(normed2, fc1_weight, preferred_element_type=jnp.float32) + fc1_bias  126 us
    dot_general x12, matrix products, contract(): return jnp.einsum(form, left, right, precision=FULL_PRECISION)  126 us
    all_to_all x1, waiting for transfers between devices, on_device(): lax.all_to_all(jnp.stack(jnp.split(imag_part, lax.axis_size('spatial'), a...  95.7 us
    all_to_all x1, waiting for transfers between devices, on_device(): lax.all_to_all(imag_part, 'spatial', split_axis=0, concat_axis=1, tiled=T...  95.6 us
    all_to_all x1, waiting for transfers between devices, on_device(): lax.all_to_all(real_part, 'spatial', split_axis=1, concat_axis=0, tiled=T...  93.3 us
    dot_general x8, matrix products, block_product(): jnp.einsum('...bi,bio->...bo', values, weight, precision=FULL_PRECISION)  92.7 us
    add x7, other arithmetic, advance(): return (moving, summed + moving.astype(jnp.float32))  92.6 us
  transfers between devices with their start and end apart: 11, of which 11 were waited for; matrix products, arithmetic and copies ran while one was open for 3% of the time, Pallas kernels for 0%

profile of v1, /device:TPU:0, one launch (start us, length us, event | category | flops | bytes accessed | tf_op | source)
XLA Modules:
  0.0 2139.3 jit_solution(15869377531767128096)
XLA Ops:
  7.6 10.5 negate_bitcast_fusion
  31.2 7.7 all-to-all-start.1
  39.0 12.0 fusion.94
  51.0 6.3 copy.55
  57.3 95.7 %all-to-all-done.1 = f32[16,32,4,768]{3,2,1,0:T(4,128)} async-done(((f32[16,32,4,768]{3,2,1,0:T(4,128)}), f32[16,32,4,768]{3,2,1,0:T(4,128)}, u32[]{:S(2)}, u32[]{:S(2)}) %all-to-all-start.1) | async-done | bytes 6291488 | tf_op jit(solution)/shard_map/all_to_all | solution.py:143
  153.0 28.5 %all-to-all-start = ((f32[32,64,768]{2,0,1:T(8,128)}), f32[32,64,768]{2,0,1:T(8,128)}, u32[]{:S(2)}, u32[]{:S(2)}) async-start(f32[32,64,768]{2,0,1:T(8,128)} %copy.55), calls=%async_computation | async-start | bytes 12582912 | tf_op jit(solution)/shard_map/all_to_all | solution.py:141
  181.6 10.3 fusion.74
  191.8 10.4 fusion.76
  202.2 93.3 %all-to-all-done = f32[32,64,768]{2,0,1:T(8,128)} async-done(((f32[32,64,768]{2,0,1:T(8,128)}), f32[32,64,768]{2,0,1:T(8,128)}, u32[]{:S(2)}, u32[]{:S(2)}) %all-to-all-start) | async-done | bytes 6291488 | tf_op jit(solution)/shard_map/all_to_all | solution.py:141
  302.0 7.9 subtract_bitcast_fusion.1
  309.8 9.9 reshape.97
  319.8 13.7 fusion.58
  333.5 9.9 fusion.60
  343.4 8.2 add_bitcast_fusion.1
  351.6 9.9 reshape.96
  361.4 13.1 add_maximum_fusion
  374.6 9.5 fusion.50
  384.1 9.8 fusion.52
  394.0 9.6 add_maximum_fusion.1
  403.6 14.9 select_bitcast_fusion
  418.5 11.0 copy.66
  429.5 9.6 reshape.99
  439.1 12.2 select_bitcast_fusion.1
  451.4 11.0 copy.65
  462.3 9.6 reshape.98
  471.9 8.3 fusion.144
  480.2 8.7 subtract_bitcast_fusion
  489.4 6.6 copy.68
  496.1 28.2 %all-to-all-start.2 = ((f32[512,4,768]{2,1,0:T(4,128)}), f32[512,4,768]{2,1,0:T(4,128)}, u32[]{:S(2)}, u32[]{:S(2)}) async-start(f32[512,4,768]{2,1,0:T(4,128)} %copy.68), calls=%async_computation.2 | async-start | bytes 12582912 | tf_op jit(solution)/shard_map/all_to_all | solution.py:156
  524.3 8.6 fusion.142
  533.0 6.7 add_bitcast_fusion
  540.1 6.7 copy.72
  546.8 91.5 %all-to-all-done.2 = f32[512,4,768]{2,1,0:T(4,128)} async-done(((f32[512,4,768]{2,1,0:T(4,128)}), f32[512,4,768]{2,1,0:T(4,128)}, u32[]{:S(2)}, u32[]{:S(2)}) %all-to-all-start.2) | async-done | bytes 6291488 | tf_op jit(solution)/shard_map/all_to_all | solution.py:156
  638.4 28.5 %all-to-all-start.3 = ((f32[512,4,768]{2,1,0:T(4,128)}), f32[512,4,768]{2,1,0:T(4,128)}, u32[]{:S(2)}, u32[]{:S(2)}) async-start(f32[512,4,768]{2,1,0:T(4,128)} %copy.72), calls=%async_computation.3 | async-start | bytes 12582912 | tf_op jit(solution)/shard_map/all_to_all | solution.py:157
  670.9 6.7 copy.70
  677.7 7.7 all_to_all.47
  685.4 95.6 %all-to-all-done.3 = f32[512,4,768]{2,1,0:T(4,128)} async-done(((f32[512,4,768]{2,1,0:T(4,128)}), f32[512,4,768]{2,1,0:T(4,128)}, u32[]{:S(2)}, u32[]{:S(2)}) %all-to-all-start.3) | async-done | bytes 6291488 | tf_op jit(solution)/shard_map/all_to_all | solution.py:157
  785.0 6.7 copy.74
  791.7 7.9 all_to_all.51
  799.6 15.1 fusion.150
  814.8 19.1 fusion.278
  838.5 126.4 %fusion.2.clone.6 = bf16[4096,3072]{1,0:T(8,128)(2,1)} fusion(bf16[4096,768]{1,0:T(8,128)(2,1)S(1)} %fusion.47, bf16[768,3072]{1,0:T(8,128)(2,1)} %param.24, f32[3072]{0:T(1024)S(1)} %copy-done.22), kind=kOutput, calls=%fused_computation.4.clone.clone.clone.clone.clone.1 | convolution fusion | flops 20157825024 | bytes 36188160 | tf_op jit(solution)/shard_map/dot_general | solution.py:163
  964.9 26.3 %fusion.49 = bf16[4096,768]{1,0:T(8,128)(2,1)S(1)} fusion(f32[32,128,768]{2,1,0:T(8,128)} %copy-done, bf16[3072,768]{1,0:T(8,128)(2,1)} %param.26, f32[768]{0:T(1024)S(1)} %copy-done.23, bf16[4096,3072]{1,0:T(8,128)(2,1)} %fusion.2.clone.6), kind=kOutput, calls=%fused_computation.62 | convolution fusion | flops 19336790016 | bytes 48761856 | tf_op jit(solution)/shard_map/dot_general | solution.py:166
  1000.0 1127.6 %while.12 = (s32[]{:T(128)}, bf16[32,128,768]{2,1,0:T(8,128)(2,1)}, f32[32,128,768]{2,1,0:T(8,128)}, s32[]{:T(128)}) while((s32[]{:T(128)}, bf16[32,128,768]{2,1,0:T(8,128)(2,1)}, f32[32,128,768]{2,1,0:T(8,128)}, s32[]{:T(128)}) %tuple.26), condition=%wide.region_5.6_spmd, body=%wide.region_4.5_spmd.sunk | while | flops 6291458 | bytes 69206104 | solution.py:177
  1000.3 9.1 collective-permute-start
  1009.3 154.1 %collective-permute-done = bf16[32,128,768]{2,1,0:T(8,128)(2,1)} collective-permute-done((bf16[32,128,768]{2,1,0:T(8,128)(2,1)}, bf16[32,128,768]{2,1,0:T(8,128)(2,1)}, u32[]{:S(2)}, u32[]{:S(2)}) %collective-permute-start) | collective-permute-done | bytes 6291488 | tf_op jit(solution)/shard_map/while/body/eval_jaxpr/ppermute | solution.py:16
  1163.4 6.1 copy.127
  1169.5 13.2 convert_add_fusion.3
  1182.8 140.2 %collective-permute-done = bf16[32,128,768]{2,1,0:T(8,128)(2,1)} collective-permute-done((bf16[32,128,768]{2,1,0:T(8,128)(2,1)}, bf16[32,128,768]{2,1,0:T(8,128)(2,1)}, u32[]{:S(2)}, u32[]{:S(2)}) %collective-permute-start) | collective-permute-done | bytes 6291488 | tf_op jit(solution)/shard_map/while/body/eval_jaxpr/ppermute | solution.py:16
  1323.0 6.1 copy.127
  1329.1 13.2 convert_add_fusion.3
  1342.4 139.4 %collective-permute-done = bf16[32,128,768]{2,1,0:T(8,128)(2,1)} collective-permute-done((bf16[32,128,768]{2,1,0:T(8,128)(2,1)}, bf16[32,128,768]{2,1,0:T(8,128)(2,1)}, u32[]{:S(2)}, u32[]{:S(2)}) %collective-permute-start) | collective-permute-done | bytes 6291488 | tf_op jit(solution)/shard_map/while/body/eval_jaxpr/ppermute | solution.py:16
  1481.8 6.1 copy.127
  1487.9 13.2 convert_add_fusion.3
  1501.1 138.5 %collective-permute-done = bf16[32,128,768]{2,1,0:T(8,128)(2,1)} collective-permute-done((bf16[32,128,768]{2,1,0:T(8,128)(2,1)}, bf16[32,128,768]{2,1,0:T(8,128)(2,1)}, u32[]{:S(2)}, u32[]{:S(2)}) %collective-permute-start) | collective-permute-done | bytes 6291488 | tf_op jit(solution)/shard_map/while/body/eval_jaxpr/ppermute | solution.py:16
  1645.8 13.2 convert_add_fusion.3
  1659.0 137.7 %collective-permute-done = bf16[32,128,768]{2,1,0:T(8,128)(2,1)} collective-permute-done((bf16[32,128,768]{2,1,0:T(8,128)(2,1)}, bf16[32,128,768]{2,1,0:T(8,128)(2,1)}, u32[]{:S(2)}, u32[]{:S(2)}) %collective-permute-start) | collective-permute-done | bytes 6291488 | tf_op jit(solution)/shard_map/while/body/eval_jaxpr/ppermute | solution.py:16
  1796.7 6.1 copy.127
  1802.9 13.2 convert_add_fusion.3
  1816.1 136.8 %collective-permute-done = bf16[32,128,768]{2,1,0:T(8,128)(2,1)} collective-permute-done((bf16[32,128,768]{2,1,0:T(8,128)(2,1)}, bf16[32,128,768]{2,1,0:T(8,128)(2,1)}, u32[]{:S(2)}, u32[]{:S(2)}) %collective-permute-start) | collective-permute-done | bytes 6291488 | tf_op jit(solution)/shard_map/while/body/eval_jaxpr/ppermute | solution.py:16
  1959.1 13.2 convert_add_fusion.3
  1972.3 136.0 %collective-permute-done = bf16[32,128,768]{2,1,0:T(8,128)(2,1)} collective-permute-done((bf16[32,128,768]{2,1,0:T(8,128)(2,1)}, bf16[32,128,768]{2,1,0:T(8,128)(2,1)}, u32[]{:S(2)}, u32[]{:S(2)}) %collective-permute-start) | collective-permute-done | bytes 6291488 | tf_op jit(solution)/shard_map/while/body/eval_jaxpr/ppermute | solution.py:16
  2114.4 13.2 convert_add_fusion.3
  2127.6 11.2 subtract_convert_fusion
  (121 shorter events, 67.3 us)
Async XLA Ops:
  0.6 4.6 copy-start.3
  0.6 7.0 copy-start.16
  0.7 7.0 copy-start.18
  5.2 33.7 %copy-start.10 = (f32[32,128]{1,0:T(8,128)}, f32[32,128]{1,0:T(8,128)S(1)}, u32[]{:S(2)}) copy-start(f32[32,128]{1,0:T(8,128)S(1)} %broadcast_multiply_fusion.1) | copy-start | bytes 49156
  7.6 31.3 %copy-start.12 = (f32[32,128]{1,0:T(8,128)}, f32[32,128]{1,0:T(8,128)S(1)}, u32[]{:S(2)}) copy-start(f32[32,128]{1,0:T(8,128)S(1)} %add_rsqrt_fusion) | copy-start | bytes 49156
  31.2 121.7 %all-to-all-start.1 = ((f32[16,32,4,768]{3,2,1,0:T(4,128)}), f32[16,32,4,768]{3,2,1,0:T(4,128)}, u32[]{:S(2)}, u32[]{:S(2)}) async-start(f32[16,32,4,768]{3,2,1,0:T(4,128)} %fusion.99), calls=%async_computation.1 | async-start | bytes 12582912 | tf_op jit(solution)/shard_map/all_to_all | solution.py:143
  57.3 124.2 %copy-start.14 = (f32[2,8,96]{2,1,0:T(8,128)S(1)}, f32[2,8,96]{2,1,0:T(8,128)}, u32[]{:S(2)}) copy-start(f32[2,8,96]{2,1,0:T(8,128)} %param.19) | copy-start | bytes 18436
  57.3 124.2 %copy-start.15 = (f32[2,8,96]{2,1,0:T(8,128)S(1)}, f32[2,8,96]{2,1,0:T(8,128)}, u32[]{:S(2)}) copy-start(f32[2,8,96]{2,1,0:T(8,128)} %param.21) | copy-start | bytes 18436
  153.0 142.6 %all-to-all-start = ((f32[32,64,768]{2,0,1:T(8,128)}), f32[32,64,768]{2,0,1:T(8,128)}, u32[]{:S(2)}, u32[]{:S(2)}) async-start(f32[32,64,768]{2,0,1:T(8,128)} %copy.55), calls=%async_computation | async-start | bytes 12582912 | tf_op jit(solution)/shard_map/all_to_all | solution.py:141
  202.2 99.7 %slice-start.10 = ((s8[6291456]{0:T(1024)(128)(4,1)}), s8[2097152]{0:T(1024)(128)(4,1)S(1)}, s32[]{:S(2)}) async-start(s8[6291456]{0:T(1024)(128)(4,1)} %bitcast.263), calls=%async_computation.14 | async-start | bytes 4194304
  295.6 6.4 slice-start.11
  299.2 2.7 copy-start.5
  309.8 9.9 copy-start.6
  319.8 13.7 copy-start.1
  319.8 23.6 %slice-start.4 = ((s8[6291456]{0:T(1024)(128)(4,1)}), s8[4194304]{0:T(1024)(128)(4,1)S(1)}, s32[]{:S(2)}) async-start(s8[6291456]{0:T(1024)(128)(4,1)} %bitcast.252), calls=%async_computation.8 | async-start | bytes 8388608
  319.8 23.6 %slice-start.8 = ((s8[6291456]{0:T(1024)(128)(4,1)}), s8[4194304]{0:T(1024)(128)(4,1)S(1)}, s32[]{:S(2)}) async-start(s8[6291456]{0:T(1024)(128)(4,1)} %bitcast.261), calls=%async_computation.12 | async-start | bytes 8388608
  333.5 9.9 slice-start.5
  333.5 9.9 slice-start.9
  361.4 13.2 copy-start.7
  374.6 9.5 copy-start.8
  374.6 19.3 slice-start
  374.6 19.3 slice-start.6
  384.1 9.9 slice-start.1
  384.1 9.9 slice-start.7
  403.6 14.9 copy-start.2
  429.5 9.6 copy-start.9
  496.1 36.9 %slice-start.2 = ((s8[6291456]{0:T(1024)(128)(4,1)}), s8[2097152]{0:T(1024)(128)(4,1)S(1)}, s32[]{:S(2)}) async-start(s8[6291456]{0:T(1024)(128)(4,1)} %bitcast.245), calls=%async_computation.6 | async-start | bytes 4194304
  496.1 142.3 %all-to-all-start.2 = ((f32[512,4,768]{2,1,0:T(4,128)}), f32[512,4,768]{2,1,0:T(4,128)}, u32[]{:S(2)}, u32[]{:S(2)}) async-start(f32[512,4,768]{2,1,0:T(4,128)} %copy.68), calls=%async_computation.2 | async-start | bytes 12582912 | tf_op jit(solution)/shard_map/all_to_all | solution.py:156
  524.3 8.6 slice-start.3
  638.4 142.6 %all-to-all-start.3 = ((f32[512,4,768]{2,1,0:T(4,128)}), f32[512,4,768]{2,1,0:T(4,128)}, u32[]{:S(2)}, u32[]{:S(2)}) async-start(f32[512,4,768]{2,1,0:T(4,128)} %copy.72), calls=%async_computation.3 | async-start | bytes 12582912 | tf_op jit(solution)/shard_map/all_to_all | solution.py:157
  799.6 15.2 copy-start.11
  799.6 15.2 copy-start.13
  799.6 15.2 copy-start.17
  799.6 15.2 copy-start.19
  833.9 4.6 copy-start
  833.9 1.5 copy-start.20
  833.9 1.5 copy-start.21
  835.5 3.1 copy-start.22
  838.5 126.4 %copy-start.23 = (f32[768]{0:T(1024)S(1)}, f32[768]{0:T(1024)}, u32[]{:S(2)}) copy-start(f32[768]{0:T(1024)} %param.27) | copy-start | bytes 9220
  991.1 8.9 copy-start.4
  1000.3 163.1 %collective-permute-start = (bf16[32,128,768]{2,1,0:T(8,128)(2,1)}, bf16[32,128,768]{2,1,0:T(8,128)(2,1)}, u32[]{:S(2)}, u32[]{:S(2)}) collective-permute-start(bf16[32,128,768]{2,1,0:T(8,128)(2,1)} %get-tuple-element.58), channel_id=1, source_target_pairs={{14,0},{15,1},{0,2},{1,3},{2,4},{3,5},{4,6},{5,7},{6,8},{7,9},{8,1... | collective-permute-start | bytes 18874376 | tf_op jit(solution)/shard_map/while/body/eval_jaxpr/ppermute | solution.py:16
  1182.8 140.2 %collective-permute-start = (bf16[32,128,768]{2,1,0:T(8,128)(2,1)}, bf16[32,128,768]{2,1,0:T(8,128)(2,1)}, u32[]{:S(2)}, u32[]{:S(2)}) collective-permute-start(bf16[32,128,768]{2,1,0:T(8,128)(2,1)} %get-tuple-element.58), channel_id=1, source_target_pairs={{14,0},{15,1},{0,2},{1,3},{2,4},{3,5},{4,6},{5,7},{6,8},{7,9},{8,1... | collective-permute-start | bytes 18874376 | tf_op jit(solution)/shard_map/while/body/eval_jaxpr/ppermute | solution.py:16
  1342.4 139.4 %collective-permute-start = (bf16[32,128,768]{2,1,0:T(8,128)(2,1)}, bf16[32,128,768]{2,1,0:T(8,128)(2,1)}, u32[]{:S(2)}, u32[]{:S(2)}) collective-permute-start(bf16[32,128,768]{2,1,0:T(8,128)(2,1)} %get-tuple-element.58), channel_id=1, source_target_pairs={{14,0},{15,1},{0,2},{1,3},{2,4},{3,5},{4,6},{5,7},{6,8},{7,9},{8,1... | collective-permute-start | bytes 18874376 | tf_op jit(solution)/shard_map/while/body/eval_jaxpr/ppermute | solution.py:16
  1501.1 138.5 %collective-permute-start = (bf16[32,128,768]{2,1,0:T(8,128)(2,1)}, bf16[32,128,768]{2,1,0:T(8,128)(2,1)}, u32[]{:S(2)}, u32[]{:S(2)}) collective-permute-start(bf16[32,128,768]{2,1,0:T(8,128)(2,1)} %get-tuple-element.58), channel_id=1, source_target_pairs={{14,0},{15,1},{0,2},{1,3},{2,4},{3,5},{4,6},{5,7},{6,8},{7,9},{8,1... | collective-permute-start | bytes 18874376 | tf_op jit(solution)/shard_map/while/body/eval_jaxpr/ppermute | solution.py:16
  1659.0 137.7 %collective-permute-start = (bf16[32,128,768]{2,1,0:T(8,128)(2,1)}, bf16[32,128,768]{2,1,0:T(8,128)(2,1)}, u32[]{:S(2)}, u32[]{:S(2)}) collective-permute-start(bf16[32,128,768]{2,1,0:T(8,128)(2,1)} %get-tuple-element.58), channel_id=1, source_target_pairs={{14,0},{15,1},{0,2},{1,3},{2,4},{3,5},{4,6},{5,7},{6,8},{7,9},{8,1... | collective-permute-start | bytes 18874376 | tf_op jit(solution)/shard_map/while/body/eval_jaxpr/ppermute | solution.py:16
  1816.1 136.8 %collective-permute-start = (bf16[32,128,768]{2,1,0:T(8,128)(2,1)}, bf16[32,128,768]{2,1,0:T(8,128)(2,1)}, u32[]{:S(2)}, u32[]{:S(2)}) collective-permute-start(bf16[32,128,768]{2,1,0:T(8,128)(2,1)} %get-tuple-element.58), channel_id=1, source_target_pairs={{14,0},{15,1},{0,2},{1,3},{2,4},{3,5},{4,6},{5,7},{6,8},{7,9},{8,1... | collective-permute-start | bytes 18874376 | tf_op jit(solution)/shard_map/while/body/eval_jaxpr/ppermute | solution.py:16
  1972.3 136.0 %collective-permute-start = (bf16[32,128,768]{2,1,0:T(8,128)(2,1)}, bf16[32,128,768]{2,1,0:T(8,128)(2,1)}, u32[]{:S(2)}, u32[]{:S(2)}) collective-permute-start(bf16[32,128,768]{2,1,0:T(8,128)(2,1)} %get-tuple-element.58), channel_id=1, source_target_pairs={{14,0},{15,1},{0,2},{1,3},{2,4},{3,5},{4,6},{5,7},{6,8},{7,9},{8,1... | collective-permute-start | bytes 18874376 | tf_op jit(solution)/shard_map/while/body/eval_jaxpr/ppermute | solution.py:16
